TPU v7x, 128 devices: a whole 4x4x4 slice. The times are simulated.
128 devices in a mesh: row: 16 (over y, z), col: 8 (over x, core).
Axes of the slice: x: 4, y: 4, z: 4, core: 2. Of those that a mesh axis runs over, the one named last changes fastest.
Arguments:
- pair_list: int32 [512, 2], P(('row', 'col')), may hold values from 0 to 127, as said below
- jacobian: float32 [512, 1024, 256], P(('row', 'col'))
- damping: float32 [16384], P('row'), may hold values from 0.5 to 2
Outputs:
- factor: float32 [16384, 1024], P('row')
- trailing: float32 [16384, 16384], P('row', 'col')
Inputs may be any that keep to these rules, and one draw needn't show every extreme that they name: `pair_list`: for pair p with entries (a, b): 0 <= b < a, and a lies in block row p // 32 of 8 subapertures, that is a * 16 // 128 equals it. A pair may appear more than once.
All inputs are finite; a program needn't handle non-finite values.
Results may differ from a plain program's by a relative error of at most 0.0001.
Values sent between devices are 32-bit elements; how exact they have to be, the bound alone decides.
No kernel may reach another device: no remote copies, remote signals or barrier semaphores. Data moves between devices by JAX's collectives and lax.ppermute only.
A program may use at most 128 MiB of HBM per device.

v0:
```python
import jax
import jax.numpy as jnp
from jax import lax
from jax.sharding import PartitionSpec as P

SUBS = 128
TERMS = 128
PANEL = 512
PANELS = 2


HIGHEST_PRECISION = lax.Precision.HIGHEST


def from_root(block, axis, owner):
    block = jnp.where(lax.axis_index(axis) == owner, block, jnp.zeros_like(block))
    return lax.psum(block, axis)


def place_pairs(
    pair_ids, upper_left, upper_right, lower_right, row_base, column_base, sub_rows, sub_columns
):
    row_slots = jnp.arange(sub_rows)
    column_slots = jnp.arange(sub_columns)
    in_rows = ((pair_ids[:, 0] - row_base)[:, None] == row_slots[None, :]).astype(jnp.float32)
    first_cols = ((pair_ids[:, 0] - column_base)[:, None] == column_slots[None, :]).astype(
        jnp.float32
    )
    second_cols = ((pair_ids[:, 1] - column_base)[:, None] == column_slots[None, :]).astype(
        jnp.float32
    )
    weight_own = in_rows[:, :, None] * first_cols[:, None, :]
    weight_cross = in_rows[:, :, None] * second_cols[:, None, :]
    tile_part = jnp.einsum("pij,pst->isjt", weight_own, upper_left, precision=HIGHEST_PRECISION)
    tile_part = tile_part + jnp.einsum(
        "pij,pst->isjt", weight_cross, upper_right, precision=HIGHEST_PRECISION
    )
    stripe_part = jnp.einsum("pj,pst->jst", second_cols, lower_right, precision=HIGHEST_PRECISION)
    return (tile_part, stripe_part)


def local(pair_list, jacobian, damping):
    row_count = lax.axis_size("row")
    column_count = lax.axis_size("col")
    row_index = lax.axis_index("row")
    column_index = lax.axis_index("col")
    sub_rows = SUBS // row_count
    sub_columns = SUBS // column_count
    rows_dev = damping.shape[0]
    columns_dev = sub_columns * TERMS
    row_ratio = row_count // column_count
    row_base = row_index * sub_rows
    column_base = column_index * sub_columns
    gram_blocks = jnp.einsum("pra,prb->pab", jacobian, jacobian, precision=HIGHEST_PRECISION)
    all_pairs = lax.all_gather(pair_list, "col", axis=0, tiled=True)
    piece_grams = lax.all_gather(gram_blocks, "col", axis=0, tiled=True)
    tile_part, stripe_part = place_pairs(
        all_pairs,
        piece_grams[:, :TERMS, :TERMS],
        piece_grams[:, :TERMS, TERMS:],
        piece_grams[:, TERMS:, TERMS:],
        row_base,
        column_base,
        sub_rows,
        sub_columns,
    )
    stripe_total = lax.psum(stripe_part, "row")
    own_subaps = row_base + jnp.arange(sub_rows)
    stripe_subaps = column_base + jnp.arange(sub_columns)
    selector = (own_subaps[:, None] == stripe_subaps[None, :]).astype(jnp.float32)
    tile_part = tile_part + jnp.einsum(
        "ij,jst->isjt", selector, stripe_total, precision=HIGHEST_PRECISION
    )
    block = tile_part.reshape(rows_dev, columns_dev)
    row_global = row_index * rows_dev + jnp.arange(rows_dev)
    column_global = column_index * columns_dev + jnp.arange(columns_dev)
    block = block + jnp.where(row_global[:, None] == column_global[None, :], damping[:, None], 0.0)
    local_tiles = jnp.arange(PANEL) // TERMS
    factors = []
    for panel_index in range(PANELS):
        begin_col = panel_index * PANEL
        end_col = begin_col + PANEL
        column = block[:, begin_col:end_col]
        row_root = begin_col // rows_dev
        offset_rows = begin_col - row_root * rows_dev
        pivot_tile = from_root(column[offset_rows : offset_rows + PANEL], "row", row_root)
        symmetric = jnp.where(
            local_tiles[:, None] >= local_tiles[None, :], pivot_tile, pivot_tile.T
        )
        lower_factor = jnp.linalg.cholesky(symmetric)
        solved = jax.scipy.linalg.solve_triangular(lower_factor, column.T, lower=True).T
        inside = (row_global >= begin_col) & (row_global < end_col)
        placed = jnp.zeros_like(column).at[offset_rows : offset_rows + PANEL].set(lower_factor)
        panel_local = jnp.where(
            (row_global >= end_col)[:, None], solved, jnp.where(inside[:, None], placed, 0.0)
        )
        factor_rows = from_root(panel_local, "col", 0)
        pieces = []
        for part_index in range(row_ratio):
            pieces.append(from_root(factor_rows, "row", column_index * row_ratio + part_index))
        factor_cols = jnp.concatenate(pieces, axis=0)
        factors.append(factor_rows)

        def renew_block(current, cols_part, factor_rows=factor_rows):
            return current - jnp.dot(factor_rows, cols_part.T, precision=HIGHEST_PRECISION)

        block = renew_block(block, factor_cols)
    factor = jnp.concatenate(factors, axis=1)
    tile_rows = row_global // TERMS
    tile_columns = column_global // TERMS
    limit = PANELS * PANEL
    keep_mask = (
        (tile_rows[:, None] >= tile_columns[None, :])
        & (row_global >= limit)[:, None]
        & (column_global >= limit)[None, :]
    )
    trailing = jnp.where(keep_mask, block, 0.0)
    return (factor, trailing)


def solution(mesh):
    placed = (P(("row", "col"), None), P(("row", "col"), None, None), P("row"))
    return jax.shard_map(
        local,
        mesh=mesh,
        in_specs=placed,
        out_specs=(P("row", None), P("row", "col")),
        check_vma=False,
    )
```

profile of v0, /device:TPU:9, one launch (start us, length us, event | category | flops | bytes accessed | tf_op | source)
XLA Modules:
  0.0 1091.6 jit_solution(6603674793765366359)
XLA Ops:
  7.2 11.2 %fusion.124 = f32[4,256,256]{2,1,0:T(8,128)} fusion(f32[4,1024,256]{2,1,0:T(8,128)} %param.11), kind=kOutput, calls=%fused_computation.225 | convolution fusion | flops 3221225472 | bytes 5242880 | tf_op jit(solution)/shard_map/pra,prb->pab/dot_general | solution.py:54
  18.5 11.1 %all-gather = s32[8,4,2]{1,2,0:T(2,128)S(1)} all-gather(s32[1,4,2]{1,2,0:T(2,128)S(1)} %bitcast.159), channel_id=1, replica_groups=mesh['row'=16,'col'=8] {'col'}, dimensions={0}, use_global_device_ids=true | all-gather | bytes 288 | tf_op jit(solution)/shard_map/all_gather | solution.py:55
  29.7 41.2 %all-gather.3.cloned.1.call-done = f32[32,256,256]{2,1,0:T(8,128)} async-done(((f32[4,256,256]{2,1,0:T(8,128)}), f32[32,256,256]{2,1,0:T(8,128)}) %all-gather.3.cloned.1.call-update) | async-done | bytes 8388624 | tf_op jit(solution)/shard_map/all_gather | solution.py:56
  70.9 4.8 fusion.123
  75.7 3.0 fusion.17
  79.1 10.2 fusion.19
  89.3 74.5 %all-reduce.13.cloned.1.call-done = f32[16,128,128]{2,0,1:T(8,128)} async-done(((f32[16,128,128]{2,0,1:T(8,128)}), f32[16,128,128]{2,0,1:T(8,128)}) %all-reduce.13.cloned.1.call-update) | async-done | bytes 1048592 | tf_op jit(solution)/shard_map/psum | solution.py:67
  163.8 11.5 %bitcast_add_fusion.1 = f32[8,128,16,128]{3,2,0,1:T(8,128)S(1)} fusion(f32[128,128,8,16]{1,3,2,0:T(8,128)} %fusion.19, f32[16,8]{0,1:T(8,128)S(1)} %convert_bitcast_fusion, f32[16,128,128]{2,0,1:T(8,128)} %all-reduce.13.cloned.1.call-done, f32[32,128,128]{2,1,0:T(8,128)} %get-tuple-element.70, f32[32,16]{0,1:T(8,128)S(1)} %get-tuple-element.108, ...), kind=kOutput, calls=%fused_computation.5 | convolution fusion | flops 811601920 | bytes 19926528 | tf_op jit(solution)/shard_map/pij,pst->isjt/dot_general | solution.py:35
  176.1 2.8 bitcast_add_fusion
  179.0 3.4 copy-done.1
  186.1 84.2 %all-reduce.15.cloned.1.call-done = f32[512,512]{1,0:T(8,128)} async-done(((f32[512,512]{1,0:T(8,128)}), f32[512,512]{1,0:T(8,128)}) %all-reduce.15.cloned.1.call-update) | async-done | bytes 1048592 | tf_op jit(solution)/shard_map/psum | solution.py:17
  270.3 2.5 copy.63
  278.4 11.7 %cholesky.286 = f32[128,128]{1,0:T(8,128)S(1)} custom-call(f32[128,128]{1,0:T(8,128)S(1)} %copy.65), custom_call_target="Cholesky" | custom-call | tf_op jit(solution)/shard_map/jit(cholesky)/cholesky | solution.py:90
  290.8 9.8 custom-call.27
  303.5 11.7 %cholesky.305 = f32[128,128]{1,0:T(8,128)S(1)} custom-call(f32[128,128]{1,0:T(8,128)S(1)} %copy.67), custom_call_target="Cholesky" | custom-call | tf_op jit(solution)/shard_map/jit(cholesky)/cholesky | solution.py:90
  317.2 10.2 custom-call.28
  329.3 11.7 %cholesky.326 = f32[128,128]{1,0:T(8,128)S(1)} custom-call(f32[128,128]{1,0:T(8,128)S(1)} %copy.69), custom_call_target="Cholesky" | custom-call | tf_op jit(solution)/shard_map/jit(cholesky)/cholesky | solution.py:90
  341.7 9.8 custom-call.29
  353.1 11.9 %cholesky.343 = f32[128,128]{1,0:T(8,128)S(1)} custom-call(f32[128,128]{1,0:T(8,128)S(1)} %copy.71), custom_call_target="Cholesky" | custom-call | tf_op jit(solution)/shard_map/jit(cholesky)/cholesky | solution.py:90
  369.8 11.2 %while.6 = (s32[]{:T(128)}, f32[512,512]{1,0:T(8,128)}, s32[4,2]{0,1:T(2,128)S(1)}, f32[4,128,128]{2,1,0:T(8,128)S(1)}, s32[]{:T(128)}) while((s32[]{:T(128)}, f32[512,512]{1,0:T(8,128)}, s32[4,2]{0,1:T(2,128)S(1)}, f32[4,128,128]{2,1,0:T(8,128)S(1)}, s32[]{:T(128)}) %tuple.72), condition=%wide.while_cond.2, body=%wide.while_body.2.sunk | while | flops 2 | bytes 131181 | solution.py:91
  381.0 39.3 %custom-call.30 = f32[4,128,128]{1,2,0:T(8,128)S(1)} custom-call(f32[4,128,128]{2,1,0:T(8,128)S(1)} %get-tuple-element.42), custom_call_target="InvertDiagBlocksLowerTriangular" | custom-call | tf_op jit(solution)/shard_map/jit(_solve_triangular)/triangular_solve | solution.py:91
  423.5 2.7 convolution_subtract_fusion.1
  427.6 4.4 fusion.35
  437.1 65.4 %all-reduce.17.cloned.1.call-done = f32[1024,512]{1,0:T(8,128)} async-done(((f32[1024,512]{1,0:T(8,128)}), f32[1024,512]{1,0:T(8,128)}) %all-reduce.17.cloned.1.call-update) | async-done | bytes 2097168 | tf_op jit(solution)/shard_map/psum | solution.py:17
  502.5 4.3 broadcast_select_fusion.3
  506.9 105.3 %all-reduce.25.cloned.1.call-done = (f32[1024,512]{1,0:T(8,128)}, f32[1024,512]{1,0:T(8,128)}) async-done(((f32[1024,512]{1,0:T(8,128)}, f32[1024,512]{1,0:T(8,128)}), (f32[1024,512]{1,0:T(8,128)}, f32[1024,512]{1,0:T(8,128)})) %all-reduce.25.cloned.1.call-update) | async-done | bytes 4194320 | tf_op jit(solution)/shard_map/psum | solution.py:17
  612.2 16.3 %fusion.8 = f32[1024,2048]{1,0:T(8,128)S(1)} fusion(f32[1024,2048]{1,0:T(8,128)} %copy-done.1, f32[1024,512]{1,0:T(8,128)S(1)} %copy-done.2, f32[1024,512]{1,0:T(8,128)} %get-tuple-element.64, f32[1024,512]{1,0:T(8,128)} %get-tuple-element.65), kind=kOutput, calls=%fused_computation.16 | convolution fusion | flops 12888047616 | bytes 23068672 | tf_op jit(solution)/shard_map/dot_general | solution.py:105
  628.6 3.4 copy-done
  634.2 3.1 slice_bitcast_fusion
  637.3 80.8 %all-reduce.19.cloned.1.call-done = f32[512,512]{1,0:T(8,128)} async-done(((f32[512,512]{1,0:T(8,128)}), f32[512,512]{1,0:T(8,128)}) %all-reduce.19.cloned.1.call-update) | async-done | bytes 1048592 | tf_op jit(solution)/shard_map/psum | solution.py:17
  718.1 2.6 copy.80
  726.3 11.7 %cholesky.358 = f32[128,128]{1,0:T(8,128)S(1)} custom-call(f32[128,128]{1,0:T(8,128)S(1)} %cholesky.439), custom_call_target="Cholesky" | custom-call | tf_op jit(solution)/shard_map/jit(cholesky)/cholesky | solution.py:90
  738.2 9.8 custom-call.31
  750.5 11.9 %cholesky.377 = f32[128,128]{1,0:T(8,128)S(1)} custom-call(f32[128,128]{1,0:T(8,128)S(1)} %cholesky.443), custom_call_target="Cholesky" | custom-call | tf_op jit(solution)/shard_map/jit(cholesky)/cholesky | solution.py:90
  763.8 9.8 custom-call.32
  775.2 11.7 %cholesky.398 = f32[128,128]{1,0:T(8,128)S(1)} custom-call(f32[128,128]{1,0:T(8,128)S(1)} %cholesky.448), custom_call_target="Cholesky" | custom-call | tf_op jit(solution)/shard_map/jit(cholesky)/cholesky | solution.py:90
  787.6 9.8 custom-call.33
  798.8 11.9 %cholesky.415 = f32[128,128]{1,0:T(8,128)S(1)} custom-call(f32[128,128]{1,0:T(8,128)S(1)} %convolution_subtract_fusion.8), custom_call_target="Cholesky" | custom-call | tf_op jit(solution)/shard_map/jit(cholesky)/cholesky | solution.py:90
  815.6 11.4 %while.7 = (s32[]{:T(128)}, f32[512,512]{1,0:T(8,128)}, s32[4,2]{0,1:T(2,128)S(1)}, f32[4,128,128]{2,1,0:T(8,128)S(1)}, s32[]{:T(128)}) while((s32[]{:T(128)}, f32[512,512]{1,0:T(8,128)}, s32[4,2]{0,1:T(2,128)S(1)}, f32[4,128,128]{2,1,0:T(8,128)S(1)}, s32[]{:T(128)}) %tuple.96), condition=%wide.while_cond.2.clone, body=%wide.while_body.2.clone.sunk | while | flops 2 | bytes 131181 | solution.py:91
  827.0 39.3 %custom-call.34 = f32[4,128,128]{1,2,0:T(8,128)S(1)} custom-call(f32[4,128,128]{2,1,0:T(8,128)S(1)} %get-tuple-element.43), custom_call_target="InvertDiagBlocksLowerTriangular" | custom-call | tf_op jit(solution)/shard_map/jit(_solve_triangular)/triangular_solve | solution.py:91
  870.9 2.7 convolution_subtract_fusion
  875.1 4.4 fusion.32
  885.2 3.1 fusion.16
  888.4 65.5 %all-reduce.21.cloned.1.call-done = f32[1024,512]{1,0:T(8,128)} async-done(((f32[1024,512]{1,0:T(8,128)}), f32[1024,512]{1,0:T(8,128)}) %all-reduce.21.cloned.1.call-update) | async-done | bytes 2097168 | tf_op jit(solution)/shard_map/psum | solution.py:17
  953.9 4.3 broadcast_select_fusion.1
  958.3 4.1 pad_maximum_fusion
  962.4 101.2 %all-reduce.23.cloned.1.call-done = (f32[1024,512]{1,0:T(8,128)}, f32[1024,512]{1,0:T(8,128)}) async-done(((f32[1024,512]{1,0:T(8,128)}, f32[1024,512]{1,0:T(8,128)}), (f32[1024,512]{1,0:T(8,128)}, f32[1024,512]{1,0:T(8,128)})) %all-reduce.23.cloned.1.call-update) | async-done | bytes 4194320 | tf_op jit(solution)/shard_map/psum | solution.py:17
  1063.6 20.7 %subtract_select_fusion = f32[1024,2048]{1,0:T(8,128)} fusion(f32[1024,2048]{1,0:T(8,128)} %copy-done, s32[2048]{0:T(1024)S(1)} %add_select_fusion, s32[1024]{0:T(1024)S(1)} %add_select_fusion.1, pred[1024]{0:T(1024)(128)(4,1)S(1)} %fusion.108, pred[2048]{0:T(1024)(128)(4,1)S(1)} %fusion.98, f32[1024,512]{1,0:T(8,128)} %all-reduce.21.cloned.1.call-done, ...), kind=kOutput, calls=%fused_computation.6 | convolution fusion | flops 12896436224 | bytes 23084032 | tf_op jit(solution)/shard_map/dot_general | solution.py:105
  (157 shorter events, 84.1 us)
Async XLA Ops:
  7.2 11.4 %copy-start.11 = (s32[4,2]{0,1:T(2,128)S(1)}, s32[4,2]{0,1:T(2,128)}, u32[]{:S(2)}) copy-start(s32[4,2]{0,1:T(2,128)} %param.10) | copy-start | bytes 100
  7.2 63.8 %all-gather.3.cloned.1.call-start = ((), (), s32[]{:S(2)}) async-start(), calls=%async_computation | async-start | bytes 9437184 | tf_op jit(solution)/shard_map/all_gather | solution.py:56
  18.5 145.3 %all-reduce.13.cloned.1.call-start = ((), (), s32[]{:S(2)}) async-start(), calls=%async_computation.1 | async-start | bytes 2097152 | tf_op jit(solution)/shard_map/psum | solution.py:67
  78.8 191.5 %all-reduce.15.cloned.1.call-start = ((), (), s32[]{:S(2)}) async-start(), calls=%async_computation.2 | async-start | bytes 2097152 | tf_op jit(solution)/shard_map/psum | solution.py:17
  175.3 0.8 copy-start.10
  179.0 3.4 copy-start.1
  183.5 319.0 %all-reduce.17.cloned.1.call-start = ((), (), s32[]{:S(2)}) async-start(), calls=%async_computation.3 | async-start | bytes 4194304 | tf_op jit(solution)/shard_map/psum | solution.py:17
  277.3 1.0 copy-start.7
  329.3 40.5 %copy-start.12 = (s32[4]{0:T(128)S(1)}, s32[4]{0:T(128)}, u32[]{:S(2)}) copy-start(s32[4]{0:T(128)} %iota_multiply_fusion) | copy-start | bytes 52
  426.8 0.8 copy-start.4
  432.1 3.4 copy-start.6
  437.0 175.2 %all-reduce.25.cloned.1.call-start = ((), (), s32[]{:S(2)}) async-start(), calls=%async_computation.7 | async-start | bytes 8388608 | tf_op jit(solution)/shard_map/psum | solution.py:17
  506.8 105.4 %copy-start.2 = (f32[1024,512]{1,0:T(8,128)S(1)}, f32[1024,512]{1,0:T(8,128)}, u32[]{:S(2)}) copy-start(f32[1024,512]{1,0:T(8,128)} %all-reduce.17.cloned.1.call-done) | copy-start | bytes 6291460
  506.8 211.3 %all-reduce.19.cloned.1.call-start = ((), (), s32[]{:S(2)}) async-start(), calls=%async_computation.4 | async-start | bytes 2097152 | tf_op jit(solution)/shard_map/psum | solution.py:17
  628.5 3.4 copy-start
  633.1 320.8 %all-reduce.21.cloned.1.call-start = ((), (), s32[]{:S(2)}) async-start(), calls=%async_computation.5 | async-start | bytes 4194304 | tf_op jit(solution)/shard_map/psum | solution.py:17
  725.3 1.0 copy-start.8
  866.4 4.6 copy-start.3
  874.3 0.8 copy-start.5
  882.6 2.6 copy-start.9
  888.4 175.2 %all-reduce.23.cloned.1.call-start = ((), (), s32[]{:S(2)}) async-start(), calls=%async_computation.6 | async-start | bytes 8388608 | tf_op jit(solution)/shard_map/psum | solution.py:17
Sparse Core Ops, SparseCore 0:
  18.6 52.3 all-gather.2
  78.9 84.8 all-reduce.12
  183.6 86.6 all-reduce.14
  437.2 65.3 all-reduce.16
  506.9 105.2 all-reduce.24
  633.3 84.8 all-reduce.18
  888.5 65.3 all-reduce.20
  958.3 105.2 all-reduce.22
where the time goes:
time: 1100 us; the launch traced here: 1090 us
  waiting for transfers between devices  618 us (56%)
  other arithmetic  272 us (25%)
  matrix products  111 us (10%)
  local copies, waits for them, and re-layouts  57.9 us (5%)
  between operations  20.3 us (2%)
  blocking collectives  11.1 us (1%)
    psum x6, waiting for transfers between devices, from_root(): return lax.psum(block, axis)  502 us
    another operation x30, other arithmetic, local(): lower_factor = jnp.linalg.cholesky(symmetric)  160 us
    another operation x3, other arithmetic, local(): jax.scipy.linalg.solve_triangular(lower_factor, column.T, lower=True)  79.1 us
    psum x1, waiting for transfers between devices, local(): stripe_total = lax.psum(stripe_part, 'row')  74.5 us
    all_gather x1, waiting for transfers between devices, local(): piece_grams = lax.all_gather(gram_blocks, 'col', axis=0, tiled=True)  41.2 us
    dot_general x2, matrix products, renew_block(): jnp.dot(factor_rows, cols_part.T, precision=HIGHEST_PRECISION)  37.1 us
    another operation x33, local copies, waits for them, and re-layouts, local(): jax.scipy.linalg.solve_triangular(lower_factor, column.T, lower=True)  28.3 us
    another operation x14, matrix products, local(): jax.scipy.linalg.solve_triangular(lower_factor, column.T, lower=True)  26.4 us
  transfers between devices with their start and end apart: 8, of which 8 were waited for; matrix products, arithmetic and copies ran while one was open for 2% of the time, Pallas kernels for 0%

commit v1 on v0

v1 whole, which is shorter than its diff:
```python
import jax
import jax.numpy as jnp
from jax import lax
from jax.experimental import pallas as pl
from jax.experimental.pallas import tpu as pltpu
from jax.sharding import PartitionSpec as P

F32 = jnp.float32
BF16 = jnp.bfloat16
HI = lax.Precision.HIGHEST
BOTH = ("row", "col")
NROW, NCOL = 16, 8
NDEV = NROW * NCOL
TILE = 128
LEAD = 8
SLOTS1 = 16
SLOTS2 = 48
DAMP_SLOT = 36
DIAG_SLOT = 40
VMEM = pltpu.VMEM
SMEM = pltpu.SMEM


def nt(a, b, precision=None):
    return lax.dot_general(
        a, b, (((1,), (1,)), ((), ())), precision=precision, preferred_element_type=F32
    )


def tn(a, b, precision=None):
    return lax.dot_general(
        a, b, (((0,), (0,)), ((), ())), precision=precision, preferred_element_type=F32
    )


def split(x):
    high = x.astype(BF16)
    return high, (x - high.astype(F32)).astype(BF16)


def nt3(ah, al, bh, bl):
    return nt(ah, bh) + (nt(ah, bl) + nt(al, bh))


def first_tile(b):
    return b * LEAD - (b * (b - 1)) // 2


def gram_kernel(jac_ref, idx_ref, damp_ref, pay_ref, cross_ref):
    q = pl.program_id(0)
    high, low = split(jac_ref[0])
    mixed = tn(high, low)
    gram = tn(high, high) + (mixed + mixed.T)
    pay_ref[pl.ds(q, TILE, stride=SLOTS1), :] = gram[:TILE, :TILE]
    pay_ref[pl.ds(q + 4, TILE, stride=SLOTS1), :] = gram[TILE:, TILE:]
    pay_ref[pl.ds(q + 8, TILE, stride=SLOTS1), :] = gram[:TILE, TILE:]
    cross_ref[0] = gram[:TILE, TILE:]

    @pl.when(q == 0)
    def _():
        pay_ref[pl.ds(12, TILE, stride=SLOTS1), :] = jnp.broadcast_to(idx_ref[...], (TILE, TILE))
        wide = jnp.concatenate([damp_ref[...], jnp.zeros((TILE - 8, TILE), F32)], axis=0)
        pay_ref[pl.ds(13, TILE, stride=SLOTS1), :] = wide.T
        zero = jnp.zeros((TILE, TILE), F32)
        pay_ref[pl.ds(14, TILE, stride=SLOTS1), :] = zero
        pay_ref[pl.ds(15, TILE, stride=SLOTS1), :] = zero


def grams(jacobian, idx, damp):
    return pl.pallas_call(
        gram_kernel,
        grid=(4,),
        in_specs=[
            pl.BlockSpec((1, 1024, 256), lambda q: (q, 0, 0)),
            pl.BlockSpec((1, TILE), lambda q: (0, 0)),
            pl.BlockSpec((8, TILE), lambda q: (0, 0)),
        ],
        out_specs=[
            pl.BlockSpec((TILE * SLOTS1, TILE), lambda q: (0, 0)),
            pl.BlockSpec((1, TILE, TILE), lambda q: (q, 0, 0)),
        ],
        out_shape=[
            jax.ShapeDtypeStruct((TILE * SLOTS1, TILE), F32),
            jax.ShapeDtypeStruct((4, TILE, TILE), F32),
        ],
        name="grams",
    )(jacobian, idx, damp)


def gather_kernel(recv_ref, pay_ref, idx_ref):
    lane = lax.broadcasted_iota(jnp.int32, (TILE, TILE), 1)
    sub = lax.broadcasted_iota(jnp.int32, (TILE, TILE), 0)
    index = recv_ref[pl.ds(12, NDEV, stride=SLOTS1), :].astype(jnp.int32)
    idx_ref[...] = index
    across = recv_ref[pl.ds(12, NDEV, stride=SLOTS1), :].T.astype(jnp.int32)
    diag = jnp.zeros((TILE, TILE), F32)
    lead = jnp.zeros((40, TILE), F32)
    sub40 = lax.broadcasted_iota(jnp.int32, (40, TILE), 0)
    lane40 = lax.broadcasted_iota(jnp.int32, (40, TILE), 1)
    for q in range(4):
        a = across[2 * q : 2 * q + 1, :]
        b = across[2 * q + 1 : 2 * q + 2, :]
        first = recv_ref[pl.ds(q, NDEV, stride=SLOTS1), :]
        second = recv_ref[pl.ds(q + 4, NDEV, stride=SLOTS1), :]
        cross = recv_ref[pl.ds(q + 8, NDEV, stride=SLOTS1), :]
        diag = diag + jnp.dot((sub == a).astype(F32), first, precision=HI)
        diag = diag + jnp.dot((sub == b).astype(F32), second, precision=HI)
        place = first_tile(b) + (a - b)
        hit = (sub40 == place) & (lane40 < NCOL)
        lead = lead + jnp.dot(hit.astype(F32), cross, precision=HI)
    hit = (sub40 == first_tile(lane40)) & (lane40 < LEAD)
    lead = lead + jnp.dot(hit.astype(F32), diag, precision=HI)
    damp = jnp.broadcast_to(recv_ref[13:14, :], (40, TILE))
    lead = jnp.where(sub40 == DAMP_SLOT, damp, lead)
    for r in range(NROW):
        for c in range(NCOL):
            base = (r * NCOL + c) * SLOTS2
            pay_ref[base : base + 40, :] = lead
            pay_ref[base + 40 : base + 48, :] = diag[8 * r : 8 * r + 8, :]


def gather_rows(recv):
    return pl.pallas_call(
        gather_kernel,
        out_shape=[
            jax.ShapeDtypeStruct((NDEV * SLOTS2, TILE), F32),
            jax.ShapeDtypeStruct((NDEV, TILE), jnp.int32),
        ],
        name="gather_rows",
    )(recv)


def factor128(rows):
    lane = lax.broadcasted_iota(jnp.int32, (8, TILE), 1)
    sub = lax.broadcasted_iota(jnp.int32, (8, TILE), 0)
    block = list(rows)
    inv = [jnp.where(lane == sub + 8 * v, 1.0, 0.0) for v in range(16)]
    upper, inverse = [], []

    def row(x, i):
        return jnp.broadcast_to(x[i : i + 1, :], (8, TILE))

    def col(x, i):
        return jnp.broadcast_to(x[:, i : i + 1], (8, TILE))

    for t in range(16):
        cols = [col(block[t], 8 * t + k) for k in range(8)]
        left, right = block[t], inv[t]
        up = jnp.zeros((8, TILE), F32)
        low, recip = up, up
        for j in range(8):
            pivot = row(cols[j], j)
            root = lax.rsqrt(pivot)
            over = 1.0 / pivot
            hit = sub == j
            scale = jnp.where(hit, 0.0, cols[j] * over)
            left_row, right_row = row(left, j), row(right, j)
            up = jnp.where(hit, left_row * root, up)
            low = jnp.where(hit, right_row * root, low)
            recip = jnp.where(hit, over, recip)
            for k in range(j + 1, 8):
                cols[k] = cols[k] - scale * row(cols[k], j)
            left = left - scale * left_row
            right = right - scale * right_row
        upper.append(jnp.where(lane >= sub + 8 * t, up, 0.0))
        inverse.append(low)
        if t < 15:
            left, right = left * recip, right * recip
            lefts = [row(left, j) for j in range(8)]
            rights = [row(right, j) for j in range(8)]
            for v in range(t + 1, 16):
                parts = [col(block[v], 8 * t + k) for k in range(8)]
                one = [parts[k] * lefts[k] for k in range(8)]
                two = [parts[k] * rights[k] for k in range(8)]
                while len(one) > 1:
                    one = [one[i] + one[i + 1] for i in range(0, len(one), 2)]
                    two = [two[i] + two[i + 1] for i in range(0, len(two), 2)]
                block[v] = block[v] - one[0]
                inv[v] = inv[v] - two[0]
    return upper, inverse


def at(i, n=TILE):
    return pl.ds(pl.multiple_of(i * n, n), n)


def factor_kernel(scal_ref, recv_ref, cross_ref, x_ref, l_ref, inv_ref, body):
    place = 0
    for k in range(LEAD):
        for i in range(k):
            body[TILE * i : TILE * (i + 1), TILE * k : TILE * (k + 1)] = jnp.zeros((TILE, TILE), F32)
        for i in range(k, LEAD):
            tile = recv_ref[pl.ds(place, TILE, stride=SLOTS2), :]
            if i == k:
                damp = recv_ref[pl.ds(DAMP_SLOT, TILE, stride=SLOTS2), :]
                lane = lax.broadcasted_iota(jnp.int32, (TILE, TILE), 1)
                sub = lax.broadcasted_iota(jnp.int32, (TILE, TILE), 0)
                tile = tile + jnp.where(lane == sub, damp[:, k : k + 1], 0.0)
            body[TILE * i : TILE * (i + 1), TILE * k : TILE * (k + 1)] = tile
            place += 1

    def clear(i, _):
        body[pl.ds(pl.multiple_of(1024 + 32 * i, 32), 32), :] = jnp.zeros((32, 1024), F32)
        return 0

    lax.fori_loop(0, 32, clear, 0)
    row = scal_ref[192]

    def fill(p, _):
        a = scal_ref[2 * p] - LEAD * row
        b = scal_ref[2 * p + 1]

        @pl.when(b < LEAD)
        def _():
            body[at(LEAD + a), at(b)] += cross_ref[at(p), :]

        return 0

    lax.fori_loop(0, 32, fill, 0)

    def step(k, _):
        rows = [
            body[pl.ds(pl.multiple_of(k * TILE + 8 * v, 8), 8), at(k)] for v in range(16)
        ]
        upper, inverse = factor128(rows)
        inv = jnp.concatenate(inverse, axis=0)
        inv_ref[at(k), :] = inv
        lower = jnp.concatenate(upper, axis=0).T

        def panel(i, _):
            x = nt(body[at(i, 256), at(k)], inv, HI)
            index = i * 256 + lax.broadcasted_iota(jnp.int32, (256, TILE), 0)
            body[at(i, 256), at(k)] = jnp.where(index >= (k + 1) * TILE, x, 0.0)
            return 0

        lax.fori_loop(0, 8, panel, 0)

        def update(j, _):
            right = body[at(j), at(k)]

            def rows_of(i, _):
                body[at(i, 512), at(j)] -= nt(body[at(i, 512), at(k)], right, HI)
                return 0

            lax.fori_loop(0, 4, rows_of, 0)
            return 0

        lax.fori_loop(k + 1, LEAD, update, 0)
        body[at(k), at(k)] = lower
        return 0

    lax.fori_loop(0, LEAD, step, 0)

    def out(i, _):
        part = pl.ds(pl.multiple_of(32 * i, 32), 32)
        below = pl.ds(pl.multiple_of(1024 + 32 * i, 32), 32)
        l_ref[part, :] = body[part, :]
        x_ref[part, :] = jnp.where(row == 0, body[part, :], body[below, :])
        return 0

    lax.fori_loop(0, 32, out, 0)


def factorise(scal, recv, cross):
    return pl.pallas_call(
        factor_kernel,
        in_specs=[
            pl.BlockSpec(memory_space=SMEM),
            pl.BlockSpec(memory_space=VMEM),
            pl.BlockSpec(memory_space=VMEM),
        ],
        out_specs=[pl.BlockSpec(memory_space=VMEM)] * 3,
        out_shape=[
            jax.ShapeDtypeStruct((1024, 1024), F32),
            jax.ShapeDtypeStruct((1024, 1024), F32),
            jax.ShapeDtypeStruct((1024, TILE), F32),
        ],
        scratch_shapes=[VMEM((2048, 1024), F32)],
        compiler_params=pltpu.CompilerParams(vmem_limit_bytes=48 * 1024 * 1024),
        cost_estimate=pl.CostEstimate(
            flops=60_000_000_000, bytes_accessed=20_000_000, transcendentals=0
        ),
        name="factorise",
    )(scal, recv, cross)


def schur_kernel(
    scal_ref, x_ref, l_ref, inv_ref, col_ref, cross_ref, diag_ref, damp_ref, out_ref,
    colx, lh, ll, xh, xl, ch, cl,
):
    step = pl.program_id(0)
    row = scal_ref[192]
    column = scal_ref[193]

    @pl.when(step == 0)
    def _():
        def clear(i, _):
            colx[at(i, 32), :] = jnp.zeros((32, 1024), F32)
            return 0

        lax.fori_loop(0, 64, clear, 0)

        def fill(p, _):
            a = scal_ref[64 + 2 * p] - 16 * column
            b = scal_ref[64 + 2 * p + 1]

            @pl.when(b < LEAD)
            def _():
                colx[at(a), at(b)] += col_ref[at(p), :]

            return 0

        lax.fori_loop(0, 64, fill, 0)

        def parts(i, _):
            lh[at(i), :], ll[at(i), :] = split(l_ref[at(i), :])
            xh[at(i), :], xl[at(i), :] = split(x_ref[at(i), :])
            return 0

        lax.fori_loop(0, 8, parts, 0)
        for k in range(LEAD):
            here = slice(TILE * k, TILE * (k + 1))
            wh, wl = split(inv_ref[here, :])

            def solve(i, _):
                rest = colx[at(i, 512), here]
                if k:
                    rest = rest - nt3(
                        ch[at(i, 512), : TILE * k],
                        cl[at(i, 512), : TILE * k],
                        lh[here, : TILE * k],
                        ll[here, : TILE * k],
                    )
                rh, rl = split(rest)
                ch[at(i, 512), here], cl[at(i, 512), here] = split(nt3(rh, rl, wh, wl))
                return 0

            lax.fori_loop(0, 4, solve, 0)

    first = 16 * column + 2 * step
    live = (row >= 1) & (first + 1 >= LEAD) & (first <= LEAD * row + 7)

    @pl.when(jnp.logical_not(live))
    def _():
        out_ref[...] = jnp.zeros_like(out_ref)

    @pl.when(live)
    def _():
        def part(i, _):
            prod = nt3(
                xh[at(i, 256), :], xl[at(i, 256), :], ch[at(step, 256), :], cl[at(step, 256), :]
            )
            tile_row = LEAD * row + 2 * i + lax.broadcasted_iota(jnp.int32, (256, 256), 0) // TILE
            tile_col = first + lax.broadcasted_iota(jnp.int32, (256, 256), 1) // TILE
            keep = (tile_row >= tile_col) & (tile_col >= LEAD)
            out_ref[at(i, 256), :] = jnp.where(keep, -prod, 0.0)
            return 0

        lax.fori_loop(0, 4, part, 0)

        def fill(p, _):
            a = scal_ref[2 * p] - LEAD * row
            b = scal_ref[2 * p + 1]

            @pl.when((b >= LEAD) & (b >= first) & (b < first + 2))
            def _():
                out_ref[at(a), at(b - first)] += cross_ref[at(p), :]

            return 0

        lax.fori_loop(0, 32, fill, 0)
        for s in range(LEAD):
            b = LEAD * row + s

            @pl.when((b >= first) & (b < first + 2))
            def _(s=s, b=b):
                lane = lax.broadcasted_iota(jnp.int32, (TILE, TILE), 1)
                sub = lax.broadcasted_iota(jnp.int32, (TILE, TILE), 0)
                damp = jnp.broadcast_to(damp_ref[s : s + 1, :], (TILE, TILE))
                tile = diag_ref[pl.ds(DIAG_SLOT + s, TILE, stride=SLOTS2), :]
                out_ref[TILE * s : TILE * (s + 1), at(b - first)] += tile + jnp.where(
                    lane == sub, damp, 0.0
                )


def schur(scal, x, lower, inv, col_cross, cross, recv, damp):
    whole = pl.BlockSpec(memory_space=VMEM)
    return pl.pallas_call(
        schur_kernel,
        grid=(8,),
        in_specs=[pl.BlockSpec(memory_space=SMEM)] + [whole] * 7,
        out_specs=pl.BlockSpec((1024, 256), lambda s: (0, s)),
        out_shape=jax.ShapeDtypeStruct((1024, 2048), F32),
        scratch_shapes=[
            VMEM((2048, 1024), F32),
            VMEM((1024, 1024), BF16),
            VMEM((1024, 1024), BF16),
            VMEM((1024, 1024), BF16),
            VMEM((1024, 1024), BF16),
            VMEM((2048, 1024), BF16),
            VMEM((2048, 1024), BF16),
        ],
        compiler_params=pltpu.CompilerParams(vmem_limit_bytes=60 * 1024 * 1024),
        cost_estimate=pl.CostEstimate(
            flops=20_000_000_000, bytes_accessed=30_000_000, transcendentals=0
        ),
        name="schur",
    )(scal, x, lower, inv, col_cross, cross, recv, damp)


def spread(x, axis, size):
    wide = jnp.broadcast_to(x[None], (size,) + x.shape)
    return lax.all_to_all(wide, axis, 0, 0, tiled=True)


def local(pair_list, jacobian, damping):
    row = lax.axis_index("row")
    column = lax.axis_index("col")
    idx = jnp.zeros((1, TILE), F32).at[0, :8].set(pair_list.reshape(8).astype(F32))
    damp = damping.reshape(8, TILE)
    payload, cross = grams(jacobian, idx, damp)
    recv = lax.all_to_all(payload.reshape(NDEV, SLOTS1, TILE), BOTH, 0, 0, tiled=True)
    payload, index = gather_rows(recv.reshape(NDEV * SLOTS1, TILE))
    recv = lax.all_to_all(payload.reshape(NDEV, SLOTS2, TILE), BOTH, 0, 0, tiled=True)
    recv = recv.reshape(NDEV * SLOTS2, TILE)

    row_cross = spread(cross.reshape(512, TILE), "col", NCOL).reshape(32 * TILE, TILE)
    moves = [
        (r * NCOL + c, (NCOL * (r % 2) + c) * NCOL + r // 2) for r in range(NROW) for c in range(NCOL)
    ]
    moved = lax.ppermute(cross.reshape(512, TILE), BOTH, moves)
    col_cross = spread(moved, "row", NROW).reshape(64 * TILE, TILE)

    index = index[:, :8].reshape(NDEV * 8)
    scal = jnp.concatenate(
        [
            lax.dynamic_slice(index, (row * 64,), (64,)),
            lax.dynamic_slice(index, (column * 128,), (128,)),
            jnp.stack([row, column]).astype(jnp.int32),
        ]
    )
    factor, lower, inv = factorise(scal, recv, row_cross)
    trailing = schur(scal, factor, lower, inv, col_cross, row_cross, recv, damp)
    return factor, trailing


def solution(mesh):
    placed = (P(("row", "col"), None), P(("row", "col"), None, None), P("row"))
    return jax.shard_map(
        local,
        mesh=mesh,
        in_specs=placed,
        out_specs=(P("row", None), P("row", "col")),
        check_vma=False,
    )
```

time: 1100 us -> 308 us (0.28)
  waiting for transfers between devices: 618 us -> 62.4 us
  other arithmetic: 272 us -> 2.05 us
  Pallas kernels: 0 us -> 178 us
  matrix products: 111 us -> 0 us
  local copies, waits for them, and re-layouts: 57.9 us -> 10.7 us
  starting transfers between devices: 1.13 us -> 25.4 us
  between operations: 20.3 us -> 0.71 us
  blocking collectives: 11.1 us -> 28.3 us
    psum x7 -> x0, waiting for transfers between devices: 577 us -> none  [the longest x6 502 us: from_root(): return lax.psum(block, axis)]
    another operation x34 -> x2, other arithmetic: 240 us -> 1.97 us  [the longest x30 160 us: local(): lower_factor = jnp.linalg.cholesky(symmetric)]
    pallas_call x0 -> x4, Pallas kernels: none -> 178 us  [the longest x1 104 us: factorise(): pl.pallas_call(factor_kernel, in_specs=[pl.BlockSpec(memory_space=SMEM),...]
    dot_general x6 -> x0, matrix products: 73 us -> none  [the longest x2 37.1 us: renew_block(): jnp.dot(factor_rows, cols_part.T, precision=HIGHEST_PRECISION)]
    all_gather x1 -> x0, waiting for transfers between devices: 41.2 us -> none  [local(): piece_grams = lax.all_gather(gram_blocks, 'col', axis=0, tiled=True)]
    ppermute x0 -> x1, waiting for transfers between devices: none -> 40.5 us  [local(): moved = lax.ppermute(cross.reshape(512, TILE), BOTH, moves)]
    another operation x26 -> x0, matrix products: 37.8 us -> none  [the longest x14 26.4 us: local(): jax.scipy.linalg.solve_triangular(lower_factor, column.T, lower=True)]
    another operation x45 -> x2, local copies, waits for them, and re-layouts: 28.9 us -> 0.18 us  [the longest x33 28.3 us: local(): jax.scipy.linalg.solve_triangular(lower_factor, column.T, lower=True)]
  transfers between devices with their start and end apart: 8 -> 4, of which waited for: 8 -> 2; matrix products, arithmetic and copies ran while one was open for 2% -> 0% of each run, Pallas kernels for 0% -> 35%
where the time goes in v1:
time: 308 us; the launch traced here: 307 us
  Pallas kernels  178 us (58%)
  waiting for transfers between devices  62.4 us (20%)
  blocking collectives  28.3 us (9%)
  starting transfers between devices  25.4 us (8%)
  local copies, waits for them, and re-layouts  10.7 us (3%)
    pallas_call x1, Pallas kernels, factorise(): pl.pallas_call(factor_kernel, in_specs=[pl.BlockSpec(memory_space=SMEM),...  104 us
    pallas_call x1, Pallas kernels, schur(): pl.pallas_call(schur_kernel, grid=(8,), in_specs=[pl.BlockSpec(memory_spa...  63.4 us
    ppermute x1, waiting for transfers between devices, local(): moved = lax.ppermute(cross.reshape(512, TILE), BOTH, moves)  40.5 us
    all_to_all x1, blocking collectives, local(): lax.all_to_all(payload.reshape(NDEV, SLOTS1, TILE), BOTH, 0, 0, tiled=True)  28.3 us
    all_to_all x2, waiting for transfers between devices, spread(): return lax.all_to_all(wide, axis, 0, 0, tiled=True)  22 us
    all_to_all x2, starting transfers between devices, spread(): return lax.all_to_all(wide, axis, 0, 0, tiled=True)  15 us
  transfers between devices with their start and end apart: 4, of which 2 were waited for; matrix products, arithmetic and copies ran while one was open for 0% of the time, Pallas kernels for 35%

profile of v1, /device:TPU:9, one launch (start us, length us, event | category | flops | bytes accessed | tf_op | source)
XLA Modules:
  0.0 307.2 jit_solution(9775323164870216792)
XLA Ops:
  0.6 0.6 compare_reduce_fusion
  1.3 1.3 convert_select_fusion
  2.6 0.1 copy.6
  2.7 0.1 reshape.75
  2.8 0.5 scatter.4.idx_ref
  3.3 5.4 %grams.1 = (f32[2048,128]{1,0:T(8,128)}, f32[4,128,128]{2,1,0:T(8,128)}) custom-call(f32[4,1024,256]{2,1,0:T(8,128)} %jac_ref.1, f32[1,128]{1,0:T(1,128)} %scatter.4.idx_ref, f32[8,128]{1,0:T(8,128)} %bitcast.21), custom_call_target="tpu_custom_call" | custom-call | tf_op jit(solution)/shard_map/grams/pallas_call | solution.py:70
  8.7 28.3 %all_to_all.20 = f32[128,16,128]{2,1,0:T(8,128)} all-to-all(f32[128,16,128]{2,1,0:T(8,128)} %bitcast.17), channel_id=1, replica_groups=mesh['row'=16,'col'=8] {'row','col'}, dimensions={0} | all-to-all | bytes 2097152 | tf_op jit(solution)/shard_map/all_to_all | solution.py:422
  37.0 2.4 broadcast_in_dim.7
  39.4 4.8 %all-to-all-start.2 = ((f32[8,512,128]{2,1,0:T(8,128)}), f32[8,512,128]{2,1,0:T(8,128)S(1)}, u32[]{:S(2)}, u32[]{:S(2)}) async-start(f32[8,512,128]{2,1,0:T(8,128)} %broadcast_in_dim.7), calls=%async_computation.2 | async-start | bytes 4194304 | tf_op jit(solution)/shard_map/all_to_all | solution.py:413
  44.2 0.0 copy-start.5
  44.2 4.3 %gather_rows.1 = (f32[6144,128]{1,0:T(8,128)}, s32[128,128]{1,0:T(8,128)}) custom-call(f32[2048,128]{1,0:T(8,128)} %bitcast.15), custom_call_target="tpu_custom_call" | custom-call | tf_op jit(solution)/shard_map/gather_rows/pallas_call | solution.py:123
  48.5 0.0 copy-start.6
  48.5 22.0 %all-to-all-done.2 = f32[8,512,128]{2,1,0:T(8,128)S(1)} async-done(((f32[8,512,128]{2,1,0:T(8,128)}), f32[8,512,128]{2,1,0:T(8,128)S(1)}, u32[]{:S(2)}, u32[]{:S(2)}) %all-to-all-start.2) | async-done | bytes 2097184 | tf_op jit(solution)/shard_map/all_to_all | solution.py:413
  70.4 0.0 copy-start.1
  70.4 1.5 copy-done.1
  71.9 6.0 %all-to-all-start.1 = ((f32[128,48,128]{2,1,0:T(8,128)}), f32[128,48,128]{2,1,0:T(8,128)S(1)}, u32[]{:S(2)}, u32[]{:S(2)}) async-start(f32[128,48,128]{2,1,0:T(8,128)} %bitcast.16), calls=%async_computation.1 | async-start | bytes 6291456 | tf_op jit(solution)/shard_map/all_to_all | solution.py:424
  77.9 0.0 copy-done.5
  77.9 4.5 %collective-permute-start = (f32[512,128]{1,0:T(8,128)S(1)}, f32[512,128]{1,0:T(8,128)}, u32[]{:S(2)}, u32[]{:S(2)}) collective-permute-start(f32[512,128]{1,0:T(8,128)S(1)} %bitcast.19), channel_id=1, source_target_pairs={{0,0},{1,8},{2,16},{3,24},{4,32},{5,40},{6,48},{7,56},{8,64},{9,72... | collective-permute-start | bytes 786440 | tf_op jit(solution)/shard_map/ppermute | solution.py:431
  82.4 0.0 copy-done.6
  82.4 0.1 reshape.79
  82.5 0.1 dynamic_slice.7
  82.6 0.1 dynamic_slice.6
  82.6 0.1 pad_add_fusion.scal_ref
  82.7 0.0 copy-start.3
  82.7 40.5 %collective-permute-done = f32[512,128]{1,0:T(8,128)} collective-permute-done((f32[512,128]{1,0:T(8,128)S(1)}, f32[512,128]{1,0:T(8,128)}, u32[]{:S(2)}, u32[]{:S(2)}) %collective-permute-start) | collective-permute-done | bytes 262176 | tf_op jit(solution)/shard_map/ppermute | solution.py:431
  123.2 0.0 all-to-all-done.1
  123.2 0.0 copy-start
  123.2 3.5 %broadcast_in_dim.16 = f32[16,512,128]{2,1,0:T(8,128)} broadcast(f32[512,128]{1,0:T(8,128)} %collective-permute-done), dimensions={1,2} | broadcast | bytes 4456448 | tf_op jit(solution)/shard_map/broadcast_in_dim | solution.py:412
  126.7 10.2 %all-to-all-start.3 = ((f32[16,512,128]{2,1,0:T(8,128)}), f32[16,512,128]{2,1,0:T(8,128)}, u32[]{:S(2)}, u32[]{:S(2)}) async-start(f32[16,512,128]{2,1,0:T(8,128)} %broadcast_in_dim.16), calls=%async_computation.3 | async-start | bytes 8388608 | tf_op jit(solution)/shard_map/all_to_all | solution.py:413
  136.9 0.0 copy-done.3
  136.9 0.0 copy-done
  136.9 0.0 copy-start.2
  136.9 1.6 copy-done.2
  138.5 104.4 %factorise.1 = (f32[1024,1024]{1,0:T(8,128)}, f32[1024,1024]{1,0:T(8,128)}, f32[1024,128]{1,0:T(8,128)S(1)}) custom-call(s32[194]{0:T(256)S(1)} %pad_add_fusion.scal_ref, f32[6144,128]{1,0:T(8,128)S(1)} %bitcast.11, f32[4096,128]{1,0:T(8,128)S(1)} %bitcast.14), custom_call_target="tpu_custom_call" | custom-call | flops 60000002048 | bytes 20000000 | tf_op jit(solution)/shard_map/factorise/pallas_call | solution.py:265
  242.9 0.0 copy-start.4
  242.9 0.8 copy-done.4
  243.7 0.0 all-to-all-done.3
  243.7 63.4 %schur.1 = f32[1024,2048]{1,0:T(8,128)} custom-call(s32[194]{0:T(256)} %copy-done.3, f32[1024,1024]{1,0:T(8,128)} %get-tuple-element.19.x_ref, f32[1024,1024]{1,0:T(8,128)} %get-tuple-element.26.l_ref, f32[1024,128]{1,0:T(8,128)} %copy-done.4, f32[8192,128]{1,0:T(8,128)} %bitcast.9.col_ref, f32[4096,128]{1,0:T(8,128)} %bitcast.13, f32[6144,128]{1,0:T(8,128)} %bitcast.12, ...), custom_call_target="tpu_custom_call" | custom-call | flops 20000000000 | bytes 30000000 | tf_op jit(solution)/shard_map/schur/pallas_call | solution.py:388
Async XLA Ops:
  39.4 31.0 %all-to-all-start.2 = ((f32[8,512,128]{2,1,0:T(8,128)}), f32[8,512,128]{2,1,0:T(8,128)S(1)}, u32[]{:S(2)}, u32[]{:S(2)}) async-start(f32[8,512,128]{2,1,0:T(8,128)} %broadcast_in_dim.7), calls=%async_computation.2 | async-start | bytes 4194304 | tf_op jit(solution)/shard_map/all_to_all | solution.py:413
  44.2 33.7 %copy-start.5 = (f32[4,128,128]{2,1,0:T(8,128)S(1)}, f32[4,128,128]{2,1,0:T(8,128)}, u32[]{:S(2)}) copy-start(f32[4,128,128]{2,1,0:T(8,128)} %get-tuple-element.24) | copy-start | bytes 786436
  48.5 33.9 %copy-start.6 = (s32[128,128]{1,0:T(8,128)S(1)}, s32[128,128]{1,0:T(8,128)}, u32[]{:S(2)}) copy-start(s32[128,128]{1,0:T(8,128)} %get-tuple-element.22) | copy-start | bytes 196612
  70.4 1.5 copy-start.1
  71.9 51.3 %all-to-all-start.1 = ((f32[128,48,128]{2,1,0:T(8,128)}), f32[128,48,128]{2,1,0:T(8,128)S(1)}, u32[]{:S(2)}, u32[]{:S(2)}) async-start(f32[128,48,128]{2,1,0:T(8,128)} %bitcast.16), calls=%async_computation.1 | async-start | bytes 6291456 | tf_op jit(solution)/shard_map/all_to_all | solution.py:424
  77.9 45.3 %collective-permute-start = (f32[512,128]{1,0:T(8,128)S(1)}, f32[512,128]{1,0:T(8,128)}, u32[]{:S(2)}, u32[]{:S(2)}) collective-permute-start(f32[512,128]{1,0:T(8,128)S(1)} %bitcast.19), channel_id=1, source_target_pairs={{0,0},{1,8},{2,16},{3,24},{4,32},{5,40},{6,48},{7,56},{8,64},{9,72... | collective-permute-start | bytes 786440 | tf_op jit(solution)/shard_map/ppermute | solution.py:431
  82.7 54.2 %copy-start.3 = (s32[194]{0:T(256)}, s32[194]{0:T(256)S(1)}, u32[]{:S(2)}) copy-start(s32[194]{0:T(256)S(1)} %pad_add_fusion.scal_ref) | copy-start | bytes 2332
  123.2 13.7 %copy-start = (f32[128,48,128]{2,1,0:T(8,128)}, f32[128,48,128]{2,1,0:T(8,128)S(1)}, u32[]{:S(2)}) copy-start(f32[128,48,128]{2,1,0:T(8,128)S(1)} %all-to-all-done.1) | copy-start | bytes 9437188
  126.7 117.0 %all-to-all-start.3 = ((f32[16,512,128]{2,1,0:T(8,128)}), f32[16,512,128]{2,1,0:T(8,128)}, u32[]{:S(2)}, u32[]{:S(2)}) async-start(f32[16,512,128]{2,1,0:T(8,128)} %broadcast_in_dim.16), calls=%async_computation.3 | async-start | bytes 8388608 | tf_op jit(solution)/shard_map/all_to_all | solution.py:413
  136.9 1.6 copy-start.2
  242.9 0.8 copy-start.4

commit v2 on v1

v2 whole, which is shorter than its diff:
```python
import jax
import jax.numpy as jnp
from jax import lax
from jax.experimental import pallas as pl
from jax.experimental.pallas import tpu as pltpu
from jax.sharding import PartitionSpec as P

F32 = jnp.float32
BF16 = jnp.bfloat16
HI = lax.Precision.HIGHEST
BOTH = ("row", "col")
NROW, NCOL = 16, 8
NDEV = NROW * NCOL
TILE = 128
LEAD = 8
SLOTS1 = 16
SLOTS2 = 48
DAMP_SLOT = 36
DIAG_SLOT = 40
VMEM = pltpu.VMEM
SMEM = pltpu.SMEM


def nt(a, b, precision=None):
    return lax.dot_general(
        a, b, (((1,), (1,)), ((), ())), precision=precision, preferred_element_type=F32
    )


def tn(a, b, precision=None):
    return lax.dot_general(
        a, b, (((0,), (0,)), ((), ())), precision=precision, preferred_element_type=F32
    )


def split(x):
    high = x.astype(BF16)
    return high, (x - high.astype(F32)).astype(BF16)


def nt3(ah, al, bh, bl):
    return nt(ah, bh) + (nt(ah, bl) + nt(al, bh))


def first_tile(b):
    return b * LEAD - (b * (b - 1)) // 2


def gram_kernel(jac_ref, idx_ref, damp_ref, pay_ref, cross_ref):
    q = pl.program_id(0)
    high, low = split(jac_ref[0])
    mixed = tn(high, low)
    gram = tn(high, high) + (mixed + mixed.T)
    pay_ref[pl.ds(q, TILE, stride=SLOTS1), :] = gram[:TILE, :TILE]
    pay_ref[pl.ds(q + 4, TILE, stride=SLOTS1), :] = gram[TILE:, TILE:]
    pay_ref[pl.ds(q + 8, TILE, stride=SLOTS1), :] = gram[:TILE, TILE:]
    cross_ref[0] = gram[:TILE, TILE:]

    @pl.when(q == 0)
    def _():
        lane = lax.broadcasted_iota(jnp.int32, (TILE, TILE), 1)
        index = jnp.zeros((TILE, TILE), F32)
        for e in range(8):
            index = jnp.where(lane == e, idx_ref[e].astype(F32), index)
        pay_ref[pl.ds(12, TILE, stride=SLOTS1), :] = index
        wide = jnp.concatenate([damp_ref[...], jnp.zeros((TILE - 8, TILE), F32)], axis=0)
        pay_ref[pl.ds(13, TILE, stride=SLOTS1), :] = wide.T
        zero = jnp.zeros((TILE, TILE), F32)
        pay_ref[pl.ds(14, TILE, stride=SLOTS1), :] = zero
        pay_ref[pl.ds(15, TILE, stride=SLOTS1), :] = zero


def grams(jacobian, idx, damp):
    return pl.pallas_call(
        gram_kernel,
        grid=(4,),
        in_specs=[
            pl.BlockSpec((1, 1024, 256), lambda q: (q, 0, 0)),
            pl.BlockSpec(memory_space=SMEM),
            pl.BlockSpec((8, TILE), lambda q: (0, 0)),
        ],
        out_specs=[
            pl.BlockSpec((TILE * SLOTS1, TILE), lambda q: (0, 0)),
            pl.BlockSpec((1, TILE, TILE), lambda q: (q, 0, 0)),
        ],
        out_shape=[
            jax.ShapeDtypeStruct((TILE * SLOTS1, TILE), F32),
            jax.ShapeDtypeStruct((4, TILE, TILE), F32),
        ],
        name="grams",
    )(jacobian, idx, damp)


def gather_kernel(recv_ref, pay_ref, idx_ref):
    lane = lax.broadcasted_iota(jnp.int32, (TILE, TILE), 1)
    sub = lax.broadcasted_iota(jnp.int32, (TILE, TILE), 0)
    index = recv_ref[pl.ds(12, NDEV, stride=SLOTS1), :].astype(jnp.int32)
    idx_ref[...] = index
    across = recv_ref[pl.ds(12, NDEV, stride=SLOTS1), :].T.astype(jnp.int32)
    diag = jnp.zeros((TILE, TILE), F32)
    lead = jnp.zeros((40, TILE), F32)
    sub40 = lax.broadcasted_iota(jnp.int32, (40, TILE), 0)
    lane40 = lax.broadcasted_iota(jnp.int32, (40, TILE), 1)
    for q in range(4):
        a = across[2 * q : 2 * q + 1, :]
        b = across[2 * q + 1 : 2 * q + 2, :]
        first = recv_ref[pl.ds(q, NDEV, stride=SLOTS1), :]
        second = recv_ref[pl.ds(q + 4, NDEV, stride=SLOTS1), :]
        cross = recv_ref[pl.ds(q + 8, NDEV, stride=SLOTS1), :]
        diag = diag + jnp.dot((sub == a).astype(F32), first, precision=HI)
        diag = diag + jnp.dot((sub == b).astype(F32), second, precision=HI)
        place = first_tile(b) + (a - b)
        hit = (sub40 == place) & (lane40 < NCOL)
        lead = lead + jnp.dot(hit.astype(F32), cross, precision=HI)
    hit = (sub40 == first_tile(lane40)) & (lane40 < LEAD)
    lead = lead + jnp.dot(hit.astype(F32), diag, precision=HI)
    damp = jnp.broadcast_to(recv_ref[13:14, :], (40, TILE))
    lead = jnp.where(sub40 == DAMP_SLOT, damp, lead)
    for r in range(NROW):
        for c in range(NCOL):
            base = (r * NCOL + c) * SLOTS2
            pay_ref[base : base + 40, :] = lead
            pay_ref[base + 40 : base + 48, :] = diag[8 * r : 8 * r + 8, :]


def gather_rows(recv):
    return pl.pallas_call(
        gather_kernel,
        out_shape=[
            jax.ShapeDtypeStruct((NDEV * SLOTS2, TILE), F32),
            jax.ShapeDtypeStruct((NDEV, TILE), jnp.int32),
        ],
        name="gather_rows",
    )(recv)


def factor128(rows):
    lane = lax.broadcasted_iota(jnp.int32, (8, TILE), 1)
    sub = lax.broadcasted_iota(jnp.int32, (8, TILE), 0)
    block = list(rows)
    inv = [jnp.where(lane == sub + 8 * v, 1.0, 0.0) for v in range(16)]
    upper, inverse = [], []

    def row(x, i):
        return jnp.broadcast_to(x[i : i + 1, :], (8, TILE))

    def col(x, i):
        return jnp.broadcast_to(x[:, i : i + 1], (8, TILE))

    for t in range(16):
        cols = [col(block[t], 8 * t + k) for k in range(8)]
        left, right = block[t], inv[t]
        up = jnp.zeros((8, TILE), F32)
        low, recip = up, up
        for j in range(8):
            pivot = row(cols[j], j)
            root = lax.rsqrt(pivot)
            over = 1.0 / pivot
            hit = sub == j
            scale = jnp.where(hit, 0.0, cols[j] * over)
            left_row, right_row = row(left, j), row(right, j)
            up = jnp.where(hit, left_row * root, up)
            low = jnp.where(hit, right_row * root, low)
            recip = jnp.where(hit, over, recip)
            for k in range(j + 1, 8):
                cols[k] = cols[k] - scale * row(cols[k], j)
            left = left - scale * left_row
            right = right - scale * right_row
        upper.append(jnp.where(lane >= sub + 8 * t, up, 0.0))
        inverse.append(low)
        if t < 15:
            left, right = left * recip, right * recip
            lefts = [row(left, j) for j in range(8)]
            rights = [row(right, j) for j in range(8)]
            for v in range(t + 1, 16):
                parts = [col(block[v], 8 * t + k) for k in range(8)]
                one = [parts[k] * lefts[k] for k in range(8)]
                two = [parts[k] * rights[k] for k in range(8)]
                while len(one) > 1:
                    one = [one[i] + one[i + 1] for i in range(0, len(one), 2)]
                    two = [two[i] + two[i + 1] for i in range(0, len(two), 2)]
                block[v] = block[v] - one[0]
                inv[v] = inv[v] - two[0]
    return upper, inverse


def at(i, n=TILE):
    return pl.ds(pl.multiple_of(i * n, n), n)


def three(x):
    high = x.astype(BF16)
    rest = x - high.astype(F32)
    mid = rest.astype(BF16)
    return high, mid, (rest - mid.astype(F32)).astype(BF16)


def stacks(x):
    h, m, low = three(x)
    return (
        jnp.concatenate([h, h], axis=1),
        jnp.concatenate([m, h], axis=1),
        jnp.concatenate([low, m], axis=1),
    )


def right_stacks(x):
    h, m, low = three(x)
    return jnp.concatenate([h, m], axis=1), jnp.concatenate([h, low], axis=1)


def six(pa, pb, pc, ra, rb):
    return nt(pa, ra) + (nt(pb, rb) + nt(pc, ra))


def factor_kernel(recv_ref, lh_ref, ll_ref, inv_ref, diag_ref, body, pa, pb, pc, ra, rb):
    place = 0
    lane = lax.broadcasted_iota(jnp.int32, (TILE, TILE), 1)
    sub = lax.broadcasted_iota(jnp.int32, (TILE, TILE), 0)
    damp = recv_ref[pl.ds(DAMP_SLOT, TILE, stride=SLOTS2), :]
    for k in range(LEAD):
        for i in range(k, LEAD):
            tile = recv_ref[pl.ds(place, TILE, stride=SLOTS2), :]
            if i == k:
                tile = tile + jnp.where(lane == sub, damp[:, k : k + 1], 0.0)
            body[TILE * i : TILE * (i + 1), TILE * k : TILE * (k + 1)] = tile
            place += 1
        diag_ref[TILE * k : TILE * (k + 1), :] = recv_ref[
            pl.ds(DIAG_SLOT + k, TILE, stride=SLOTS2), :
        ]

    def step(k, _):
        rows = [
            body[pl.ds(pl.multiple_of(k * TILE + 8 * v, 8), 8), at(k)] for v in range(16)
        ]
        upper, inverse = factor128(rows)
        inv = jnp.concatenate(inverse, axis=0)
        inv_ref[at(k), :] = inv
        wa, wb = right_stacks(inv)

        def panel(i, _):
            x = six(*stacks(body[at(i, 512), at(k)]), wa, wb)
            index = i * 512 + lax.broadcasted_iota(jnp.int32, (512, TILE), 0)
            x = jnp.where(index >= (k + 1) * TILE, x, 0.0)
            h, m, low = three(x)
            pa[at(i, 512), :] = jnp.concatenate([h, h], axis=1)
            pb[at(i, 512), :] = jnp.concatenate([m, h], axis=1)
            pc[at(i, 512), :] = jnp.concatenate([low, m], axis=1)
            ra[at(i, 512), :] = jnp.concatenate([h, m], axis=1)
            rb[at(i, 512), :] = jnp.concatenate([h, low], axis=1)
            lh_ref[at(i, 512), at(k)] = h
            ll_ref[at(i, 512), at(k)] = m
            return 0

        begin = (k >= 3).astype(jnp.int32)
        @pl.when(k >= 3)
        def _():
            zero = jnp.zeros((512, TILE), BF16)
            lh_ref[:512, at(k)] = zero
            ll_ref[:512, at(k)] = zero

        lax.fori_loop(begin, 2, panel, 0)

        def update(j, _):
            wa, wb = ra[at(j), :], rb[at(j), :]

            def rows_of(i, _):
                part = at(i, 512)
                body[part, at(j)] -= six(pa[part, :], pb[part, :], pc[part, :], wa, wb)
                return 0

            lax.fori_loop((j >= 4).astype(jnp.int32), 2, rows_of, 0)
            return 0

        lax.fori_loop(k + 1, LEAD, update, 0)
        lh_ref[at(k), at(k)], ll_ref[at(k), at(k)] = split(jnp.concatenate(upper, axis=0).T)
        return 0

    lax.fori_loop(0, LEAD, step, 0)


def factorise(recv):
    return pl.pallas_call(
        factor_kernel,
        in_specs=[pl.BlockSpec(memory_space=VMEM)],
        out_specs=[pl.BlockSpec(memory_space=VMEM)] * 4,
        out_shape=[
            jax.ShapeDtypeStruct((1024, 1024), BF16),
            jax.ShapeDtypeStruct((1024, 1024), BF16),
            jax.ShapeDtypeStruct((1024, TILE), F32),
            jax.ShapeDtypeStruct((1024, TILE), F32),
        ],
        scratch_shapes=[VMEM((1024, 1024), F32)] + [VMEM((1024, 256), BF16)] * 5,
        compiler_params=pltpu.CompilerParams(vmem_limit_bytes=32 * 1024 * 1024),
        cost_estimate=pl.CostEstimate(
            flops=40_000_000_000, bytes_accessed=8_000_000, transcendentals=0
        ),
        name="factorise",
    )(recv)


def schur_kernel(
    scal_ref, lh_ref, ll_ref, inv_ref, col_ref, cross_ref, diag_ref, damp_ref,
    factor_ref, out_ref, rows, ch, cl, where_ref, tiles_ref,
):
    row = scal_ref[192]
    column = scal_ref[193]
    for u in range(24):
        where_ref[u] = 0

    def mark_row(p, _):
        a = scal_ref[2 * p] - LEAD * row
        where_ref[a] = jnp.where(scal_ref[2 * p + 1] < LEAD, 1, where_ref[a])
        return 0

    def mark_col(p, _):
        tile = scal_ref[64 + 2 * p]
        a = tile - 16 * column + LEAD
        used = (scal_ref[65 + 2 * p] < LEAD) & (tile >= LEAD) & (tile <= LEAD * row + 7)
        where_ref[a] = jnp.where(used, 1, where_ref[a])
        return 0

    @pl.when(row >= 1)
    def _():
        lax.fori_loop(0, 32, mark_row, 0)
        lax.fori_loop(0, 64, mark_col, 0)

    def place(u, count):
        used = where_ref[u] == 1
        where_ref[u] = jnp.where(used, count, -1)
        tiles_ref[count] = u
        return count + used.astype(jnp.int32)

    n_row = lax.fori_loop(0, LEAD, place, jnp.int32(0))
    total = lax.fori_loop(LEAD, 24, place, n_row)

    def clear(i, _):
        rows[at(i), :] = jnp.zeros((TILE, 1024), F32)
        return 0

    lax.fori_loop(0, total, clear, 0)

    def fill_row(p, _):
        a = scal_ref[2 * p] - LEAD * row
        b = scal_ref[2 * p + 1]

        @pl.when((b < LEAD) & (where_ref[a] >= 0))
        def _():
            rows[at(where_ref[a]), at(b)] += cross_ref[at(p), :]

        return 0

    def fill_col(p, _):
        a = scal_ref[64 + 2 * p] - 16 * column + LEAD
        b = scal_ref[65 + 2 * p]

        @pl.when((b < LEAD) & (where_ref[a] >= 0))
        def _():
            rows[at(where_ref[a]), at(b)] += col_ref[at(p), :]

        return 0

    lax.fori_loop(0, 32, fill_row, 0)
    lax.fori_loop(0, 64, fill_col, 0)

    def blank(i, _):
        out_ref[at(i, 32), :] = jnp.zeros((32, 2048), F32)
        return 0

    lax.fori_loop(0, 32, blank, 0)

    def fill_out(p, _):
        a = scal_ref[2 * p] - LEAD * row
        b = scal_ref[2 * p + 1]
        here = b - 16 * column

        @pl.when((b >= LEAD) & (here >= 0) & (here < 16))
        def _():
            out_ref[at(a), at(here)] += cross_ref[at(p), :]

        return 0

    lax.fori_loop(0, 32, fill_out, 0)

    @pl.when((row >= 1) & (row // 2 == column))
    def _():
        lane = lax.broadcasted_iota(jnp.int32, (TILE, TILE), 1)
        sub = lax.broadcasted_iota(jnp.int32, (TILE, TILE), 0)
        for s in range(LEAD):
            damp = jnp.broadcast_to(damp_ref[s : s + 1, :], (TILE, TILE))
            tile = diag_ref[TILE * s : TILE * (s + 1), :] + jnp.where(lane == sub, damp, 0.0)
            out_ref[TILE * s : TILE * (s + 1), at(LEAD * (row % 2) + s)] += tile

    for k in range(LEAD):
        here = slice(TILE * k, TILE * (k + 1))
        wh, wl = split(inv_ref[here, :])

        def solve(i, _, k=k, here=here, wh=wh, wl=wl):
            rest = rows[at(i, 512), here]
            if k:
                rest = rest - nt3(
                    ch[at(i, 512), : TILE * k],
                    cl[at(i, 512), : TILE * k],
                    lh_ref[here, : TILE * k],
                    ll_ref[here, : TILE * k],
                )
            x = nt3(*split(rest), wh, wl)
            rows[at(i, 512), here] = x
            ch[at(i, 512), here], cl[at(i, 512), here] = split(x)
            return 0

        lax.fori_loop(0, (total + 3) // 4, solve, 0)

    for s in range(LEAD):
        part = slice(TILE * s, TILE * (s + 1))

        @pl.when(where_ref[s] >= 0)
        def _(s=s, part=part):
            factor_ref[part, :] = rows[at(where_ref[s]), :]

        @pl.when((where_ref[s] < 0) & (row >= 1))
        def _(part=part):
            factor_ref[part, :] = jnp.zeros((TILE, 1024), F32)

        @pl.when(row == 0)
        def _(part=part):
            factor_ref[part, :] = lh_ref[part, :].astype(F32) + ll_ref[part, :].astype(F32)

    n_col = total - n_row

    def columns(j, _):
        jt = n_row + 2 * j
        right = pl.ds(pl.multiple_of(jt * TILE, TILE), 256)

        def blocks(i, _):
            left = at(i, 256)
            prod = nt3(ch[left, :], cl[left, :], ch[right, :], cl[right, :])
            for p in range(2):
                for q in range(2):
                    it = 2 * i + p
                    a = tiles_ref[jnp.minimum(it, 23)]
                    b = tiles_ref[jnp.minimum(jt + q, 23)] - LEAD
                    keep = (it < n_row) & (jt + q < total) & (LEAD * row + a >= 16 * column + b)

                    @pl.when(keep)
                    def _(a=a, b=b, p=p, q=q):
                        out_ref[at(a), at(b)] -= prod[
                            TILE * p : TILE * (p + 1), TILE * q : TILE * (q + 1)
                        ]

            return 0

        lax.fori_loop(0, (n_row + 1) // 2, blocks, 0)
        return 0

    lax.fori_loop(0, (n_col + 1) // 2, columns, 0)


def schur(scal, lh, ll, inv, col_cross, cross, diag, damp):
    whole = pl.BlockSpec(memory_space=VMEM)
    return pl.pallas_call(
        schur_kernel,
        in_specs=[pl.BlockSpec(memory_space=SMEM)] + [whole] * 7,
        out_specs=[whole] * 2,
        out_shape=[
            jax.ShapeDtypeStruct((1024, 1024), F32),
            jax.ShapeDtypeStruct((1024, 2048), F32),
        ],
        scratch_shapes=[
            VMEM((3072, 1024), F32),
            VMEM((3328, 1024), BF16),
            VMEM((3328, 1024), BF16),
            SMEM((24,), jnp.int32),
            SMEM((25,), jnp.int32),
        ],
        compiler_params=pltpu.CompilerParams(vmem_limit_bytes=60 * 1024 * 1024),
        cost_estimate=pl.CostEstimate(
            flops=20_000_000_000, bytes_accessed=30_000_000, transcendentals=0
        ),
        name="schur",
    )(scal, lh, ll, inv, col_cross, cross, diag, damp)


def local(pair_list, jacobian, damping):
    row = lax.axis_index("row")
    column = lax.axis_index("col")
    damp = damping.reshape(8, TILE)
    payload, cross = grams(jacobian, pair_list.reshape(8), damp)
    recv = lax.all_to_all(payload.reshape(NDEV, SLOTS1, TILE), BOTH, 0, 0, tiled=True)
    payload, index = gather_rows(recv.reshape(NDEV * SLOTS1, TILE))
    recv = lax.all_to_all(payload.reshape(NDEV, SLOTS2, TILE), BOTH, 0, 0, tiled=True)
    lower_high, lower_low, inv, diag = factorise(recv.reshape(NDEV * SLOTS2, TILE))

    cross = cross.reshape(4 * TILE, TILE)
    moves = [
        (r * NCOL + c, (NCOL * (r % 2) + c) * NCOL + r // 2) for r in range(NROW) for c in range(NCOL)
    ]
    moved = lax.ppermute(cross, BOTH, moves)
    row_cross = lax.all_gather(cross, "col", axis=0, tiled=True)
    col_cross = lax.all_gather(moved, "row", axis=0, tiled=True)

    index = index[:, :8].reshape(NDEV * 8)
    scal = jnp.concatenate(
        [
            lax.dynamic_slice(index, (row * 64,), (64,)),
            lax.dynamic_slice(index, (column * 128,), (128,)),
            jnp.stack([row, column]).astype(jnp.int32),
        ]
    )
    return tuple(schur(scal, lower_high, lower_low, inv, col_cross, row_cross, diag, damp))


def solution(mesh):
    placed = (P(("row", "col"), None), P(("row", "col"), None, None), P("row"))
    return jax.shard_map(
        local,
        mesh=mesh,
        in_specs=placed,
        out_specs=(P("row", None), P("row", "col")),
        check_vma=False,
    )
```

time: 308 us -> 241 us (0.78)
  Pallas kernels: 178 us -> 129 us
  blocking collectives: 28.3 us -> 0 us
  between operations: 0.71 us -> 14.1 us
  waiting for transfers between devices: 62.4 us -> 67.5 us
  starting transfers between devices: 25.4 us -> 20.9 us
  local copies, waits for them, and re-layouts: 10.7 us -> 7.59 us
    pallas_call x2, Pallas kernels: 168 us -> 119 us  [the longest x1 63.6 us: schur(): pl.pallas_call(schur_kernel, in_specs=[pl.BlockSpec(memory_space=SMEM)] +...]
    all_to_all x1, waiting for transfers between devices: 0.01 us -> 40.6 us  [local(): lax.all_to_all(payload.reshape(NDEV, SLOTS2, TILE), BOTH, 0, 0, tiled=True)]
    ppermute x1, waiting for transfers between devices: 40.5 us -> 1.5 us  [local(): moved = lax.ppermute(cross, BOTH, moves)]
    all_to_all x1 -> x0, blocking collectives: 28.3 us -> none  [local(): lax.all_to_all(payload.reshape(NDEV, SLOTS1, TILE), BOTH, 0, 0, tiled=True)]
    broadcast_in_dim x2 -> x0, local copies, waits for them, and re-layouts: 5.94 us -> none  [spread(): wide = jnp.broadcast_to(x[None], (size,) + x.shape)]
    all_to_all x2 -> x1, starting transfers between devices: 15 us -> 9.02 us  [local(): lax.all_to_all(payload.reshape(NDEV, SLOTS1, TILE), BOTH, 0, 0, tiled=True)]
    all_to_all x2 -> x1, waiting for transfers between devices: 22 us -> 25.4 us  [local(): lax.all_to_all(payload.reshape(NDEV, SLOTS1, TILE), BOTH, 0, 0, tiled=True)]
    unnamed x14 -> x15, local copies, waits for them, and re-layouts: 3.86 us -> 6.75 us
  transfers between devices with their start and end apart: 4 -> 5, of which waited for: 2 -> 3; matrix products, arithmetic and copies ran while one was open for 0% -> 0% of each run, Pallas kernels for 35% -> 25%
where the time goes in v2:
time: 241 us; the launch traced here: 240 us
  Pallas kernels  129 us (54%)
  waiting for transfers between devices  67.5 us (28%)
  starting transfers between devices  20.9 us (9%)
  between operations  14.1 us (6%)
  local copies, waits for them, and re-layouts  7.59 us (3%)
    pallas_call x1, Pallas kernels, schur(): pl.pallas_call(schur_kernel, in_specs=[pl.BlockSpec(memory_space=SMEM)] +...  63.6 us
    pallas_call x1, Pallas kernels, factorise(): pl.pallas_call(factor_kernel, in_specs=[pl.BlockSpec(memory_space=VMEM)],...  55.9 us
    all_to_all x1, waiting for transfers between devices, local(): lax.all_to_all(payload.reshape(NDEV, SLOTS2, TILE), BOTH, 0, 0, tiled=True)  40.6 us
    all_to_all x1, waiting for transfers between devices, local(): lax.all_to_all(payload.reshape(NDEV, SLOTS1, TILE), BOTH, 0, 0, tiled=True)  25.4 us
    all_to_all x1, starting transfers between devices, local(): lax.all_to_all(payload.reshape(NDEV, SLOTS1, TILE), BOTH, 0, 0, tiled=True)  9.02 us
    all_to_all x1, starting transfers between devices, local(): lax.all_to_all(payload.reshape(NDEV, SLOTS2, TILE), BOTH, 0, 0, tiled=True)  6.93 us
    unnamed x15, local copies, waits for them, and re-layouts  6.75 us
    pallas_call x1, Pallas kernels, grams(): pl.pallas_call(gram_kernel, grid=(4,), in_specs=[pl.BlockSpec((1, 1024, 2...  5.47 us
  transfers between devices with their start and end apart: 5, of which 3 were waited for; matrix products, arithmetic and copies ran while one was open for 0% of the time, Pallas kernels for 25%

profile of v2, /device:TPU:9, one launch (start us, length us, event | category | flops | bytes accessed | tf_op | source)
XLA Modules:
  0.0 239.9 jit_solution(13211537593616549967)
XLA Ops:
  7.2 0.0 all-gather.5.cloned.1.call-start
  7.2 0.8 copy.6
  8.0 0.6 reshape.28.idx_ref
  8.6 5.5 %grams.1 = (f32[2048,128]{1,0:T(8,128)}, f32[4,128,128]{2,1,0:T(8,128)}) custom-call(f32[4,1024,256]{2,1,0:T(8,128)} %jac_ref.1, s32[8]{0:T(128)} %reshape.28.idx_ref, f32[8,128]{1,0:T(8,128)} %bitcast.16), custom_call_target="tpu_custom_call" | custom-call | tf_op jit(solution)/shard_map/grams/pallas_call | solution.py:74
  14.0 0.0 all-gather.5.cloned.1.call-update
  14.1 4.9 %collective-permute-start = (f32[512,128]{1,0:T(8,128)}, f32[512,128]{1,0:T(8,128)S(1)}, u32[]{:S(2)}, u32[]{:S(2)}) collective-permute-start(f32[512,128]{1,0:T(8,128)} %bitcast.14), channel_id=1, source_target_pairs={{0,0},{1,8},{2,16},{3,24},{4,32},{5,40},{6,48},{7,56},{8,64},{9,72... | collective-permute-start | bytes 786440 | tf_op jit(solution)/shard_map/ppermute | solution.py:498
  19.0 9.0 %all-to-all-start = ((f32[128,16,128]{2,1,0:T(8,128)}), f32[128,16,128]{2,1,0:T(8,128)S(1)}, u32[]{:S(2)}, u32[]{:S(2)}) async-start(f32[128,16,128]{2,1,0:T(8,128)} %bitcast.12), calls=%async_computation | async-start | bytes 2097152 | tf_op jit(solution)/shard_map/all_to_all | solution.py:489
  28.0 0.0 all-gather.3.cloned.1.call-start
  28.1 1.5 collective-permute-done
  29.6 0.0 copy-start.5
  29.6 0.7 copy-done.5
  30.3 0.0 all-gather.3.cloned.1.call-update
  30.3 25.4 %all-to-all-done = f32[128,16,128]{2,1,0:T(8,128)S(1)} async-done(((f32[128,16,128]{2,1,0:T(8,128)}), f32[128,16,128]{2,1,0:T(8,128)S(1)}, u32[]{:S(2)}, u32[]{:S(2)}) %all-to-all-start) | async-done | bytes 1048608 | tf_op jit(solution)/shard_map/all_to_all | solution.py:489
  55.7 0.0 copy-start.4
  55.7 1.0 copy-done.4
  56.6 4.2 %gather_rows.1 = (f32[6144,128]{1,0:T(8,128)}, s32[128,128]{1,0:T(8,128)}) custom-call(f32[2048,128]{1,0:T(8,128)} %bitcast.10), custom_call_target="tpu_custom_call" | custom-call | tf_op jit(solution)/shard_map/gather_rows/pallas_call | solution.py:127
  60.9 0.0 copy-start.6
  60.9 6.9 %all-to-all-start.1 = ((f32[128,48,128]{2,1,0:T(8,128)}), f32[128,48,128]{2,1,0:T(8,128)S(1)}, u32[]{:S(2)}, u32[]{:S(2)}) async-start(f32[128,48,128]{2,1,0:T(8,128)} %bitcast.11), calls=%async_computation.1 | async-start | bytes 6291456 | tf_op jit(solution)/shard_map/all_to_all | solution.py:491
  67.8 0.0 copy-done.6
  67.8 0.1 reshape.32
  67.9 0.1 dynamic_slice.7
  68.0 0.1 dynamic_slice.6
  68.1 0.6 pad_add_fusion.scal_ref
  68.7 40.6 %all-to-all-done.1 = f32[128,48,128]{2,1,0:T(8,128)S(1)} async-done(((f32[128,48,128]{2,1,0:T(8,128)}), f32[128,48,128]{2,1,0:T(8,128)S(1)}, u32[]{:S(2)}, u32[]{:S(2)}) %all-to-all-start.1) | async-done | bytes 3145760 | tf_op jit(solution)/shard_map/all_to_all | solution.py:491
  109.3 55.9 %factorise.1 = (bf16[1024,1024]{1,0:T(8,128)(2,1)S(1)}, bf16[1024,1024]{1,0:T(8,128)(2,1)S(1)}, f32[1024,128]{1,0:T(8,128)S(1)}, f32[1024,128]{1,0:T(8,128)S(1)}) custom-call(f32[6144,128]{1,0:T(8,128)S(1)} %bitcast.9), custom_call_target="tpu_custom_call" | custom-call | flops 40000000000 | bytes 8000000 | tf_op jit(solution)/shard_map/factorise/pallas_call | solution.py:283
  165.1 0.0 copy-start
  165.2 1.3 copy-done
  166.5 0.0 copy-start.1
  166.5 1.4 copy-done.1
  167.9 0.0 copy-start.2
  167.9 0.8 copy-done.2
  168.7 0.0 copy-start.3
  168.7 0.8 copy-done.3
  169.5 0.0 all-gather.5.cloned.1.call-done.cross_ref
  169.5 0.0 all-gather.3.cloned.1.call-done.col_ref
  169.5 63.6 %schur.1 = (f32[1024,1024]{1,0:T(8,128)}, f32[1024,2048]{1,0:T(8,128)}) custom-call(s32[194]{0:T(256)} %pad_add_fusion.scal_ref, bf16[1024,1024]{1,0:T(8,128)(2,1)} %copy-done, bf16[1024,1024]{1,0:T(8,128)(2,1)} %copy-done.1, f32[1024,128]{1,0:T(8,128)} %copy-done.2, f32[8192,128]{1,0:T(8,128)} %all-gather.3.cloned.1.call-done.col_ref, ...), custom_call_target="tpu_custom_call" | custom-call | flops 20000000000 | bytes 30000000 | tf_op jit(solution)/shard_map/schur/pallas_call | solution.py:461
Async XLA Ops:
  7.2 162.3 %all-gather.5.cloned.1.call-start = ((), (), s32[]{:S(2)}) async-start(), calls=%async_computation.3 | async-start | bytes 2359296 | tf_op jit(solution)/shard_map/all_gather | solution.py:499
  14.1 15.5 %collective-permute-start = (f32[512,128]{1,0:T(8,128)}, f32[512,128]{1,0:T(8,128)S(1)}, u32[]{:S(2)}, u32[]{:S(2)}) collective-permute-start(f32[512,128]{1,0:T(8,128)} %bitcast.14), channel_id=1, source_target_pairs={{0,0},{1,8},{2,16},{3,24},{4,32},{5,40},{6,48},{7,56},{8,64},{9,72... | collective-permute-start | bytes 786440 | tf_op jit(solution)/shard_map/ppermute | solution.py:498
  19.0 36.7 %all-to-all-start = ((f32[128,16,128]{2,1,0:T(8,128)}), f32[128,16,128]{2,1,0:T(8,128)S(1)}, u32[]{:S(2)}, u32[]{:S(2)}) async-start(f32[128,16,128]{2,1,0:T(8,128)} %bitcast.12), calls=%async_computation | async-start | bytes 2097152 | tf_op jit(solution)/shard_map/all_to_all | solution.py:489
  28.0 141.5 %all-gather.3.cloned.1.call-start = ((), (), s32[]{:S(2)}) async-start(), calls=%async_computation.2 | async-start | bytes 4456448 | tf_op jit(solution)/shard_map/all_gather | solution.py:500
  29.6 0.7 copy-start.5
  55.7 1.0 copy-start.4
  60.9 7.0 %copy-start.6 = (s32[128,128]{1,0:T(8,128)S(1)}, s32[128,128]{1,0:T(8,128)}, u32[]{:S(2)}) copy-start(s32[128,128]{1,0:T(8,128)} %get-tuple-element.11) | copy-start | bytes 196612
  60.9 48.4 %all-to-all-start.1 = ((f32[128,48,128]{2,1,0:T(8,128)}), f32[128,48,128]{2,1,0:T(8,128)S(1)}, u32[]{:S(2)}, u32[]{:S(2)}) async-start(f32[128,48,128]{2,1,0:T(8,128)} %bitcast.11), calls=%async_computation.1 | async-start | bytes 6291456 | tf_op jit(solution)/shard_map/all_to_all | solution.py:491
  165.1 1.4 copy-start
  166.5 1.4 copy-start.1
  167.9 0.8 copy-start.2
  168.7 0.8 copy-start.3
Sparse Core Ops, SparseCore 0:
  14.2 36.7 all-gather.4
  53.2 81.6 all-gather.2
